TPU v7x, 256 devices: a whole 4x4x8 slice. The times are simulated.
256 devices in a mesh: req: 64 (over x_lo, z, y), tp: 4 (over x_hi, core).
Axes of the slice: x: 4 (x_hi: 2, x_lo: 2; x = x_hi * 2 + x_lo), y: 4, z: 8, core: 2. Of those that a mesh axis runs over, the one named last changes fastest.
Arguments:
- hidden: bfloat16 [64, 512, 1280], P('req'), may hold values from -6 to 6
- membership: int32 [64], P('req'), may hold values from 0 to 3
- lengths: int32 [64], P('req'), may hold values from 8 to 512, as said below
- owners: int32 [4, 16], replicated, may hold values from 0 to 63, as said below
- prefix_cache: bfloat16 [4096, 20, 128], P('req', 'tp'), may hold values from -6 to 6
- w_query: bfloat16 [1280, 1280], P(None, 'tp'), may hold values from -0.25 to 0.25
- w_key: bfloat16 [1280, 1280], P(None, 'tp'), may hold values from -0.25 to 0.25
- w_value: bfloat16 [1280, 1280], P(None, 'tp'), may hold values from -0.15625 to 0.15625
- key_scale: float32 [20, 64], P('tp'), may hold values from 0.5 to 6
- w_out: bfloat16 [1280, 1280], P('tp'), may hold values from -0.15625 to 0.15625
- step_rates: float32 [1280], replicated, may hold values from 0.1 to 0.8
Outputs:
- layer_out: bfloat16 [64, 512, 1280], P('req', None, 'tp')
Inputs may be any that keep to these rules, and one draw needn't show every extreme that they name: `lengths`: every request has at least one suffix token; some request has length 512. `owners`: each cache slot appears exactly once in the table.
All inputs are finite; a program needn't handle non-finite values.
Results may differ from a plain program's by a relative error of at most 0.0085.
Values may be sent and summed in bfloat16 or wider, within the bound.
No kernel may reach another device: no remote copies, remote signals or barrier semaphores. Data moves between devices by JAX's collectives and lax.ppermute only.
A program may use at most 128 MiB of HBM per device.

v0:
```python
import math
import jax
import jax.numpy as jnp
from jax import lax
from jax.sharding import PartitionSpec as P


def normed(values):
    return values * lax.rsqrt(jnp.mean(values * values, axis=-1, keepdims=True) + 1e-06)


def scaled_keys(raw_keys, key_scale, head_size):
    return (normed(raw_keys.astype(jnp.float32)) * key_scale / math.sqrt(head_size)).astype(
        jnp.bfloat16
    )


def partial_attention(queries, key_rows, value_rows, visible):
    scores = jnp.einsum("qhd,khd->hqk", queries, key_rows, preferred_element_type=jnp.float32)
    masked = jnp.where(visible[None], scores, -1e30)
    row_peak = jnp.max(masked, axis=-1)
    weights = jnp.where(visible[None], jnp.exp(masked - row_peak[..., None]), 0.0)
    row_total = jnp.sum(weights, axis=-1)
    weighted = jnp.einsum(
        "hqk,khd->hqd", weights.astype(jnp.bfloat16), value_rows, preferred_element_type=jnp.float32
    )
    return (row_peak, row_total, weighted)


def combine(earlier, later_part):
    row_peak = jnp.maximum(earlier[0], later_part[0])
    scale_one = jnp.exp(earlier[0] - row_peak)
    scale_two = jnp.exp(later_part[0] - row_peak)
    return (
        row_peak,
        earlier[1] * scale_one + later_part[1] * scale_two,
        earlier[2] * scale_one[..., None] + later_part[2] * scale_two[..., None],
    )


def local(
    hidden,
    membership,
    lengths,
    owners,
    prefix_cache,
    w_query,
    w_key,
    w_value,
    key_scale,
    w_out,
    step_rates,
):
    req_count, suf_len, model_width = hidden.shape
    heads_here, head_size = key_scale.shape
    row_count = req_count * suf_len
    flat_rows = hidden.reshape(row_count, model_width)
    queries = (
        normed(
            jnp.dot(flat_rows, w_query, preferred_element_type=jnp.float32).reshape(
                req_count, suf_len, heads_here, head_size
            )
        )
        * key_scale
    ).astype(jnp.bfloat16)
    key_rows = scaled_keys(
        jnp.dot(flat_rows, w_key, preferred_element_type=jnp.float32).reshape(
            req_count, suf_len, heads_here, head_size
        ),
        key_scale,
        head_size,
    )
    value_rows = (
        jnp.dot(flat_rows, w_value, preferred_element_type=jnp.float32)
        .astype(jnp.bfloat16)
        .reshape(req_count, suf_len, heads_here, head_size)
    )
    positions = jnp.arange(suf_len)
    causal = positions[None, :] <= positions[:, None]

    def local_attention(inputs):
        query_one, keys_one, values_one, length_one = inputs
        return partial_attention(
            query_one, keys_one, values_one, causal & (positions[None, :] < length_one)
        )

    local_part = lax.map(local_attention, (queries, key_rows, value_rows, lengths))
    slot_rows = prefix_cache.shape[0]
    gathered = lax.all_gather(prefix_cache, "req", axis=0, tiled=True)
    slot_table = gathered.reshape(-1, slot_rows, heads_here, 2 * head_size)[owners]
    slot_table = slot_table.reshape(owners.shape[0], -1, heads_here, 2 * head_size)
    pre_keys = scaled_keys(slot_table[..., :head_size], key_scale, head_size)
    pre_values = slot_table[..., head_size:]
    everyone = jnp.ones((1, pre_keys.shape[1]), bool)

    def prefix_attention(inputs):
        query_one, group_one = inputs
        return partial_attention(query_one, pre_keys[group_one], pre_values[group_one], everyone)

    prefix_part = lax.map(prefix_attention, (queries, membership))
    merged = combine(prefix_part, local_part)
    attended = merged[2] / merged[1][..., None]
    attended = (
        attended.transpose(0, 2, 1, 3)
        .reshape(row_count, heads_here * head_size)
        .astype(jnp.bfloat16)
    )
    partial_out = jnp.dot(attended, w_out, preferred_element_type=jnp.float32)
    valid = (positions[None, :] < lengths[:, None]).reshape(row_count, 1)
    part_width = model_width // lax.axis_size("tp")
    offset = lax.axis_index("tp") * part_width
    summed = lax.psum(partial_out.astype(jnp.bfloat16), "tp").astype(jnp.float32)
    branch = normed(summed)
    state_rows = flat_rows.astype(jnp.float32)
    updated = normed(state_rows + step_rates * (branch - state_rows))
    result = lax.dynamic_slice_in_dim(updated, offset, part_width, 1)
    layer_out = jnp.where(valid, result, 0.0).astype(jnp.bfloat16)
    return layer_out.reshape(req_count, suf_len, part_width)


def solution(mesh):
    in_specs = (
        P("req", None, None),
        P("req"),
        P("req"),
        P(),
        P("req", "tp", None),
        P(None, "tp"),
        P(None, "tp"),
        P(None, "tp"),
        P("tp", None),
        P("tp", None),
        P(),
    )
    out_specs = P("req", None, "tp")
    return jax.shard_map(local, mesh=mesh, in_specs=in_specs, out_specs=out_specs, check_vma=False)
```

profile of v0, /device:TPU:1, one launch (start us, length us, event | category | flops | bytes accessed | tf_op | source)
XLA Modules:
  0.0 428.9 jit_solution(8274242587962377966)
XLA Ops:
  6.5 0.0 copy-start
  6.5 0.0 copy-start.2
  6.5 0.0 all-gather.2.cloned.1.call-start
  6.5 0.7 all-gather.2.cloned.1.call-update
  7.3 0.0 all-reduce.2.cloned.1.call-start
  7.3 0.7 compare_select_fusion
  8.0 0.1 reshape.221
  8.7 0.0 copy-start.3
  8.7 3.0 fusion.69
  11.8 0.1 reduce_sum.67
  11.8 2.2 fusion.67
  14.0 0.1 reduce_sum.65
  14.8 0.1 fusion.43
  14.9 0.0 copy-done.2
  14.9 1.8 fusion.40
  16.7 0.0 copy-done.3
  16.7 2.3 select_reduce_fusion
  19.0 0.0 copy-start.1
  19.0 2.4 copy-done.1
  21.4 1.1 fusion.5
  22.5 251.3 %all-gather.2.cloned.1.call-done = bf16[4096,5,128]{2,0,1:T(8,128)(2,1)} async-done(((bf16[64,5,128]{2,0,1:T(8,128)(2,1)}), bf16[4096,5,128]{2,0,1:T(8,128)(2,1)}) %all-gather.2.cloned.1.call-update) | async-done | bytes 5242896 | tf_op jit(solution)/shard_map/all_gather | solution.py:89
  273.8 6.1 %copy.23 = bf16[64,64,5,128]{3,1,2,0:T(8,128)(2,1)} copy(bf16[64,64,5,128]{3,1,0,2:T(8,128)(2,1)} %bitcast.59) | data formatting | bytes 10485760 | tf_op jit(solution)/shard_map/reshape | solution.py:90
  279.9 6.0 %gather_fusion = bf16[64,64,5,128]{3,1,2,0:T(8,128)(2,1)} fusion(bf16[64,64,5,128]{3,1,2,0:T(8,128)(2,1)} %copy.23, s32[1024]{0:T(1024)S(1)} %pad_clamp_fusion), kind=kCustom, calls=%fused_computation | custom fusion | bytes 10486016 | tf_op jit(solution)/shard_map/gather | solution.py:90
  285.9 6.4 %copy.24 = bf16[64,64,5,128]{3,1,0,2:T(8,128)(2,1)} copy(bf16[64,64,5,128]{3,1,2,0:T(8,128)(2,1)} %gather_fusion) | data formatting | bytes 10485760 | tf_op jit(solution)/shard_map/gather | solution.py:90
  292.4 11.2 %slice_convert_fusion = (f32[4,1024,5,64]{3,1,0,2:T(8,128)}, bf16[4,1024,5,64]{3,1,0,2:T(8,128)(2,1)}) fusion(bf16[4,1024,5,128]{3,1,0,2:T(8,128)(2,1)} %bitcast.53), kind=kLoop, calls=%fused_computation.6 | loop fusion | flops 1310720 | bytes 13107200 | tf_op jit(solution)/shard_map/convert_element_type | solution.py:13
  303.5 5.5 %multiply_reduce_fusion = f32[4,1024,5]{1,0,2:T(4,128)S(1)} fusion(bf16[4,1024,5,128]{3,1,0,2:T(8,128)(2,1)} %bitcast.54), kind=kLoop, calls=%fused_computation.2 | loop fusion | flops 3911680 | bytes 2703360 | tf_op jit(solution)/shard_map/reduce_sum | solution.py:9
  309.1 4.0 fusion.68
  313.0 0.0 slice-start
  313.1 2.3 fusion
  315.4 0.0 slice-start.1
  315.4 3.3 fusion.35
  318.7 0.0 slice-done
  318.7 0.0 slice-done.1
  318.7 0.0 copy-start.4
  318.7 1.6 fusion.47
  320.3 0.0 copy-done
  320.3 2.0 convolution_convert_fusion
  322.2 0.0 all-reduce.2.cloned.1.call-update
  322.3 94.6 %all-reduce.2.cloned.1.call-done = bf16[512,1280]{1,0:T(8,128)(2,1)} async-done(((bf16[512,1280]{1,0:T(8,128)(2,1)}), bf16[512,1280]{1,0:T(8,128)(2,1)}) %all-reduce.2.cloned.1.call-update) | async-done | bytes 1310736 | tf_op jit(solution)/shard_map/psum | solution.py:112
  416.8 1.6 fusion.8
  418.5 0.0 copy-done.4
  418.5 2.2 multiply_reduce_fusion.1
  420.7 0.4 fusion.52
  421.2 0.9 copy.28
  (9 shorter events, 0.1 us)
Async XLA Ops:
  6.5 313.8 %copy-start = (bf16[320,1280]{1,0:T(8,128)(2,1)S(1)}, bf16[320,1280]{1,0:T(8,128)(2,1)}, u32[]{:S(2)}) copy-start(bf16[320,1280]{1,0:T(8,128)(2,1)} %param.20) | copy-start | bytes 2457604
  6.5 8.4 %copy-start.2 = (bf16[1,512,1280]{2,1,0:T(8,128)(2,1)S(1)}, bf16[1,512,1280]{2,1,0:T(8,128)(2,1)}, u32[]{:S(2)}) copy-start(bf16[1,512,1280]{2,1,0:T(8,128)(2,1)} %param.11) | copy-start | bytes 3932164
  6.5 267.3 %all-gather.2.cloned.1.call-start = ((), (), s32[]{:S(2)}) async-start(), calls=%async_computation | async-start | bytes 5324800 | tf_op jit(solution)/shard_map/all_gather | solution.py:89
  7.3 409.6 %all-reduce.2.cloned.1.call-start = ((), (), s32[]{:S(2)}) async-start(), calls=%async_computation.1 | async-start | bytes 2621440 | tf_op jit(solution)/shard_map/psum | solution.py:112
  8.7 8.0 %copy-start.3 = (f32[5,64]{1,0:T(8,128)S(1)}, f32[5,64]{1,0:T(8,128)}, u32[]{:S(2)}) copy-start(f32[5,64]{1,0:T(8,128)} %param.19) | copy-start | bytes 3844
  19.0 2.4 copy-start.1
  313.0 5.6 %slice-start = ((s8[5242880]{0:T(1024)(128)(4,1)}), s8[4194304]{0:T(1024)(128)(4,1)S(1)}, s32[]{:S(2)}) async-start(s8[5242880]{0:T(1024)(128)(4,1)} %bitcast.55), calls=%async_computation.2 | async-start | bytes 8388608
  315.4 3.3 slice-start.1
  318.7 99.8 %copy-start.4 = (f32[1280]{0:T(1024)S(1)}, f32[1280]{0:T(1024)}, u32[]{:S(2)}) copy-start(f32[1280]{0:T(1024)} %param.21) | copy-start | bytes 15364
Sparse Core Ops, SparseCore 0:
  9.1 264.6 all-gather.1
  322.4 94.4 all-reduce.1
where the time goes:
time: 429 us
  waiting for transfers between devices  347 us (81%)
  other arithmetic  25.3 us (6%)
  local copies, waits for them, and re-layouts  21.9 us (5%)
  matrix products  20 us (5%)
  between operations  14.9 us (3%)
    all_gather x1, waiting for transfers between devices, local(): gathered = lax.all_gather(prefix_cache, 'req', axis=0, tiled=True)  251 us
    psum x1, waiting for transfers between devices, local(): lax.psum(partial_out.astype(jnp.bfloat16), 'tp').astype(jnp.float32)  94.6 us
    gather x2, local copies, waits for them, and re-layouts, local(): gathered.reshape(-1, slot_rows, heads_here, 2 * head_size)[owners]  12.4 us
    convert_element_type x1, other arithmetic, scaled_keys(): raw_keys.astype(jnp.float32)  11.2 us
    reduce_sum x5, other arithmetic, normed(): jnp.mean(values * values, axis=-1, keepdims=True) + 1e-06  9.4 us
  transfers between devices with their start and end apart: 2, of which 2 were waited for; matrix products, arithmetic and copies ran while one was open for 3% of the time, Pallas kernels for 0%

commit v1 on v0

--- a/solution.py
+++ b/solution.py
@@ -86,7 +86,9 @@
 
     local_part = lax.map(local_attention, (queries, key_rows, value_rows, lengths))
     slot_rows = prefix_cache.shape[0]
-    gathered = lax.all_gather(prefix_cache, "req", axis=0, tiled=True)
+    gathered = jnp.concatenate(
+        lax.all_to_all(jnp.stack([prefix_cache] * lax.axis_size("req")), "req", 0, 0), axis=0
+    )
     slot_table = gathered.reshape(-1, slot_rows, heads_here, 2 * head_size)[owners]
     slot_table = slot_table.reshape(owners.shape[0], -1, heads_here, 2 * head_size)
     pre_keys = scaled_keys(slot_table[..., :head_size], key_scale, head_size)

time: 429 us -> 248 us (0.58)
  waiting for transfers between devices: 347 us -> 154 us
  starting transfers between devices: 0.04 us -> 14 us
    all_gather x1 -> x0, waiting for transfers between devices: 251 us -> none  [local(): gathered = lax.all_gather(prefix_cache, 'req', axis=0, tiled=True)]
    all_to_all x0 -> x1, waiting for transfers between devices: none -> 102 us  [local(): lax.all_to_all(jnp.stack([prefix_cache] * lax.axis_size('req')), 'req', 0...]
    psum x1, waiting for transfers between devices: 94.6 us -> 52.6 us  [local(): lax.psum(partial_out.astype(jnp.bfloat16), 'tp').astype(jnp.float32)]
    all_to_all x0 -> x1, starting transfers between devices: none -> 13.9 us  [local(): lax.all_to_all(jnp.stack([prefix_cache] * lax.axis_size('req')), 'req', 0...]
    reshape x1 -> x0, local copies, waits for them, and re-layouts: 6.08 us -> none  [local(): gathered.reshape(-1, slot_rows, heads_here, 2 * head_size)[owners]]
    another operation x0 -> x1, local copies, waits for them, and re-layouts: none -> 4.65 us  [local(): jnp.stack([prefix_cache] * lax.axis_size('req'))]
  transfers between devices with their start and end apart: 2 -> 2, of which waited for: 2 -> 2; matrix products, arithmetic and copies ran while one was open for 3% -> 4% of each run, Pallas kernels for 0% -> 0%
where the time goes in v1:
time: 248 us
  waiting for transfers between devices  154 us (62%)
  other arithmetic  24.5 us (10%)
  local copies, waits for them, and re-layouts  20.5 us (8%)
  matrix products  19.4 us (8%)
  between operations  15 us (6%)
  starting transfers between devices  14 us (6%)
    all_to_all x1, waiting for transfers between devices, local(): lax.all_to_all(jnp.stack([prefix_cache] * lax.axis_size('req')), 'req', 0...  102 us
    psum x1, waiting for transfers between devices, local(): lax.psum(partial_out.astype(jnp.bfloat16), 'tp').astype(jnp.float32)  52.6 us
    all_to_all x1, starting transfers between devices, local(): lax.all_to_all(jnp.stack([prefix_cache] * lax.axis_size('req')), 'req', 0...  13.9 us
    gather x2, local copies, waits for them, and re-layouts, local(): gathered.reshape(-1, slot_rows, heads_here, 2 * head_size)[owners]  12.5 us
    convert_element_type x1, other arithmetic, scaled_keys(): raw_keys.astype(jnp.float32)  11.2 us
    reduce_sum x5, other arithmetic, normed(): jnp.mean(values * values, axis=-1, keepdims=True) + 1e-06  9.22 us
    dot_general x2, matrix products, partial_attention(): jnp.einsum('qhd,khd->hqk', queries, key_rows, preferred_element_type=jnp....  6.47 us
  transfers between devices with their start and end apart: 2, of which 2 were waited for; matrix products, arithmetic and copies ran while one was open for 4% of the time, Pallas kernels for 0%

profile of v1, /device:TPU:1, one launch (start us, length us, event | category | flops | bytes accessed | tf_op | source)
XLA Modules:
  0.0 247.7 jit_solution(14314030911828907827)
XLA Ops:
  6.5 0.0 copy-start
  6.5 4.6 %stack.2 = bf16[64,64,5,128]{3,1,2,0:T(8,128)(2,1)} broadcast(bf16[64,5,128]{2,0,1:T(8,128)(2,1)} %param.15), dimensions={1,2,3} | broadcast | bytes 5324800 | tf_op jit(solution)/shard_map/stack | solution.py:90
  11.2 0.0 copy-start.5
  11.2 0.0 copy-start.2
  11.2 13.9 %all-to-all-start = ((bf16[64,64,5,128]{3,1,2,0:T(8,128)(2,1)}), bf16[64,64,5,128]{3,1,2,0:T(8,128)(2,1)}, u32[]{:S(2)}, u32[]{:S(2)}) async-start(bf16[64,64,5,128]{3,1,2,0:T(8,128)(2,1)} %stack.2), calls=%async_computation | async-start | bytes 10485760 | tf_op jit(solution)/shard_map/all_to_all | solution.py:90
  25.1 0.0 all-reduce.2.cloned.1.call-start
  25.2 0.0 copy-done.5
  25.2 0.1 reshape.219
  25.9 0.0 copy-done.2
  25.9 0.0 copy-start.3
  26.0 2.6 %fusion.69 = (f32[512,320]{0,1:T(8,128)S(1)}, f32[512,320]{0,1:T(8,128)}) fusion(bf16[1280,320]{0,1:T(8,128)(2,1)} %param.17, bf16[1,512,1280]{2,1,0:T(8,128)(2,1)S(1)} %copy-done.2), kind=kOutput, calls=%fused_computation.79 | convolution fusion | flops 419594240 | bytes 3440640 | tf_op jit(solution)/shard_map/dot_general | solution.py:67
  28.6 0.1 reduce_sum.67
  28.7 1.8 fusion.67
  30.4 0.1 reduce_sum.65
  31.2 0.1 fusion.43
  31.3 1.8 fusion.40
  33.1 0.0 copy-done.3
  33.1 2.3 select_reduce_fusion
  35.5 0.0 copy-start.1
  35.5 2.4 copy-done.1
  37.8 1.1 fusion.5
  38.9 101.7 %all-to-all-done = bf16[64,64,5,128]{3,1,2,0:T(8,128)(2,1)} async-done(((bf16[64,64,5,128]{3,1,2,0:T(8,128)(2,1)}), bf16[64,64,5,128]{3,1,2,0:T(8,128)(2,1)}, u32[]{:S(2)}, u32[]{:S(2)}) %all-to-all-start) | async-done | bytes 5242912 | tf_op jit(solution)/shard_map/all_to_all | solution.py:90
  140.6 6.1 %gather_fusion = bf16[64,64,5,128]{3,1,2,0:T(8,128)(2,1)} fusion(bf16[64,64,5,128]{3,1,2,0:T(8,128)(2,1)} %all-to-all-done, s32[1024]{0:T(1024)S(1)} %pad_clamp_fusion), kind=kCustom, calls=%fused_computation | custom fusion | bytes 10486016 | tf_op jit(solution)/shard_map/gather | solution.py:92
  146.7 6.4 %copy.20 = bf16[64,64,5,128]{3,1,0,2:T(8,128)(2,1)} copy(bf16[64,64,5,128]{3,1,2,0:T(8,128)(2,1)} %gather_fusion) | data formatting | bytes 10485760 | tf_op jit(solution)/shard_map/gather | solution.py:92
  153.1 11.2 %slice_convert_fusion = (f32[4,1024,5,64]{3,1,0,2:T(8,128)}, bf16[4,1024,5,64]{3,1,0,2:T(8,128)(2,1)}) fusion(bf16[4,1024,5,128]{3,1,0,2:T(8,128)(2,1)} %bitcast.52), kind=kLoop, calls=%fused_computation.6 | loop fusion | flops 1310720 | bytes 13107200 | tf_op jit(solution)/shard_map/convert_element_type | solution.py:13
  164.3 5.3 %multiply_reduce_fusion = f32[4,1024,5]{1,0,2:T(4,128)S(1)} fusion(bf16[4,1024,5,128]{3,1,0,2:T(8,128)(2,1)} %bitcast.53), kind=kLoop, calls=%fused_computation.2 | loop fusion | flops 3911680 | bytes 2703360 | tf_op jit(solution)/shard_map/reduce_sum | solution.py:9
  169.6 4.1 %fusion.68 = (f32[5,512]{1,0:T(8,128)S(1)}, f32[5,512,1024]{2,1,0:T(8,128)S(1)}) fusion(f32[4,1024,5,64]{3,1,0,2:T(8,128)} %get-tuple-element.46, s32[]{:T(128)S(6)} %select_n.30, f32[5,64]{1,0:T(8,128)S(1)} %copy-done.3, f32[1,1024,5]{1,0,2:T(1,128)S(1)} %constant_dynamic-slice_fusion, f32[512,5,64]{0,2,1:T(8,128)S(1)} %bitcast.57, ...), kind=kOutput, calls=%fused_computation.78 | convolution fusion | flops 339965440 | bytes 13817860 | tf_op jit(solution)/shard_map/while/body/eval_jaxpr/qhd,khd->hqk/dot_general | solution.py:19
  173.8 0.0 slice-start
  173.8 2.3 fusion
  176.1 0.0 slice-start.1
  176.1 3.3 %fusion.35 = f32[5,512,64]{1,2,0:T(8,128)S(1)} fusion(bf16[4,1024,5,64]{3,1,0,2:T(8,128)(2,1)} %get-tuple-element.47, s32[]{:T(128)S(6)} %select_n.30, f32[5,512,1024]{2,1,0:T(8,128)S(1)} %get-tuple-element.59, f32[5,512]{1,0:T(8,128)S(1)} %get-tuple-element.58, f32[5,512]{1,0:T(8,128)S(1)} %get-tuple-element.45), kind=kOutput, calls=%fused_computation.41 | convolution fusion | flops 340951040 | bytes 12472324 | tf_op jit(solution)/shard_map/while/body/eval_jaxpr/hqk,khd->hqd/dot_general | solution.py:24
  179.4 0.0 slice-done
  179.4 0.0 slice-done.1
  179.4 0.0 copy-start.4
  179.4 1.6 fusion.47
  181.0 0.0 copy-done
  181.0 2.0 convolution_convert_fusion
  183.0 0.0 all-reduce.2.cloned.1.call-update
  183.0 52.6 %all-reduce.2.cloned.1.call-done = bf16[512,1280]{1,0:T(8,128)(2,1)} async-done(((bf16[512,1280]{1,0:T(8,128)(2,1)}), bf16[512,1280]{1,0:T(8,128)(2,1)}) %all-reduce.2.cloned.1.call-update) | async-done | bytes 1310736 | tf_op jit(solution)/shard_map/psum | solution.py:114
  235.6 1.6 fusion.8
  237.3 0.0 copy-done.4
  237.3 2.2 multiply_reduce_fusion.1
  239.5 0.4 fusion.52
  239.9 0.9 copy.24
  (10 shorter events, 0.1 us)
Async XLA Ops:
  6.5 174.5 %copy-start = (bf16[320,1280]{1,0:T(8,128)(2,1)S(1)}, bf16[320,1280]{1,0:T(8,128)(2,1)}, u32[]{:S(2)}) copy-start(bf16[320,1280]{1,0:T(8,128)(2,1)} %param.20) | copy-start | bytes 2457604
  11.2 14.0 %copy-start.5 = (s32[4,16]{1,0:T(4,128)S(1)}, s32[4,16]{1,0:T(4,128)}, u32[]{:S(2)}) copy-start(s32[4,16]{1,0:T(4,128)} %param.14) | copy-start | bytes 772
  11.2 14.8 %copy-start.2 = (bf16[1,512,1280]{2,1,0:T(8,128)(2,1)S(1)}, bf16[1,512,1280]{2,1,0:T(8,128)(2,1)}, u32[]{:S(2)}) copy-start(bf16[1,512,1280]{2,1,0:T(8,128)(2,1)} %param.11) | copy-start | bytes 3932164
  11.2 129.4 %all-to-all-start = ((bf16[64,64,5,128]{3,1,2,0:T(8,128)(2,1)}), bf16[64,64,5,128]{3,1,2,0:T(8,128)(2,1)}, u32[]{:S(2)}, u32[]{:S(2)}) async-start(bf16[64,64,5,128]{3,1,2,0:T(8,128)(2,1)} %stack.2), calls=%async_computation | async-start | bytes 10485760 | tf_op jit(solution)/shard_map/all_to_all | solution.py:90
  25.1 210.5 %all-reduce.2.cloned.1.call-start = ((), (), s32[]{:S(2)}) async-start(), calls=%async_computation.1 | async-start | bytes 2621440 | tf_op jit(solution)/shard_map/psum | solution.py:114
  25.9 7.2 %copy-start.3 = (f32[5,64]{1,0:T(8,128)S(1)}, f32[5,64]{1,0:T(8,128)}, u32[]{:S(2)}) copy-start(f32[5,64]{1,0:T(8,128)} %param.19) | copy-start | bytes 3844
  35.5 2.4 copy-start.1
  173.8 5.6 %slice-start = ((s8[5242880]{0:T(1024)(128)(4,1)}), s8[4194304]{0:T(1024)(128)(4,1)S(1)}, s32[]{:S(2)}) async-start(s8[5242880]{0:T(1024)(128)(4,1)} %bitcast.54), calls=%async_computation.2 | async-start | bytes 8388608
  176.1 3.3 %slice-start.1 = ((s8[5242880]{0:T(1024)(128)(4,1)}), s8[1048576]{0:T(1024)(128)(4,1)S(1)}, s32[]{:S(2)}) async-start(s8[5242880]{0:T(1024)(128)(4,1)} %bitcast.54), calls=%async_computation.3 | async-start | bytes 2097152
  179.4 57.9 %copy-start.4 = (f32[1280]{0:T(1024)S(1)}, f32[1280]{0:T(1024)}, u32[]{:S(2)}) copy-start(f32[1280]{0:T(1024)} %param.21) | copy-start | bytes 15364
Sparse Core Ops, SparseCore 0:
  183.1 52.4 all-reduce.1
